TPU v7x, 512 devices: a whole 4x8x8 slice. The times are simulated.
512 devices in a mesh: ep: 128 (over y, z, core), hid: 4 (over x).
Axes of the slice: x: 4, y: 8, z: 8, core: 2. Of those that a mesh axis runs over, the one named last changes fastest.
Arguments:
- attention: bfloat16 [8192, 1536], P('ep', 'hid'), may hold values from -6 to 6
- stream: bfloat16 [8192, 1536], P('ep', 'hid'), may hold values from -16 to 16
- o_weight: bfloat16 [1536, 1536], P('hid'), may hold values from -0.15625 to 0.15625
- routes: int32 [8192, 4], P('ep'), may hold values from 0 to 31, all different within a row; in each aligned block of 64 rows (0 to 63, 64 to 127, ...) at most 16 rows name the same one
- route_weight: float32 [8192, 4], P('ep'), may hold values from 0.1 to 1
- gate_up: bfloat16 [128, 1536, 2, 768], P('ep', None, None, 'hid'), as said below
- down_proj: bfloat16 [128, 768, 1536], P('ep', 'hid'), as said below
- norm_gain: float32 [1536], P('hid'), may hold values from 0.1 to 1.9
Outputs:
- stream_out: bfloat16 [8192, 1536], P('ep', 'hid')
- normed: bfloat16 [8192, 1536], P('ep', 'hid')
Inputs may be any that keep to these rules, and one draw needn't show every extreme that they name: `routes`: A row names 4 different experts. In each aligned block of 64 rows (the rows of one index of ep) no expert is named by more than 16 rows, a bound that some block reaches. `gate_up`: slot s holds the weights of expert s mod 32; all slots of one expert are equal. `down_proj`: slot s holds the weights of expert s mod 32; all slots of one expert are equal.
All inputs are finite; a program needn't handle non-finite values.
Results may differ from a plain program's by a relative error of at most 0.019.
Values may be sent and summed in bfloat16 or wider, within the bound.
A program may use at most 64 MiB of HBM per device.

v0:
```python
import jax
import jax.numpy as jnp
from jax import lax
from jax.sharding import PartitionSpec as P

EXPERTS = 32
MOST = 16


epsilon = 1e-06


def expert_hidden(rows_in, gate_cols, width):
    gate_up_out = jnp.einsum("jrd,jdf->jrf", rows_in, gate_cols, preferred_element_type=jnp.float32)
    return (jax.nn.relu(gate_up_out[..., :width]) * gate_up_out[..., width:]).astype(jnp.bfloat16)


def on_device(attention, stream, o_weight, routes, route_weight, gate_up, down_proj, norm_gain):
    groups = lax.axis_size("ep")
    hid_parts = lax.axis_size("hid")
    tok_rows, quarter = stream.shape
    top_count = routes.shape[1]
    slots_dev = gate_up.shape[0]
    group_width = gate_up.shape[3]
    replicas = slots_dev * groups // EXPERTS
    capacity = MOST // replicas
    full_width = quarter * hid_parts
    projected = jnp.dot(attention, o_weight, preferred_element_type=jnp.float32)
    summed = lax.psum_scatter(
        projected.astype(jnp.bfloat16), "hid", scatter_dimension=1, tiled=True
    ).astype(jnp.float32)
    mixed_rows = (stream.astype(jnp.float32) + summed).astype(jnp.bfloat16)
    flat_expert = routes.reshape(-1)
    flat_count = tok_rows * top_count
    onehot = (flat_expert[:, None] == jnp.arange(EXPERTS, dtype=jnp.int32)[None, :]).astype(
        jnp.int32
    )
    row_rank = jnp.sum((jnp.cumsum(onehot, axis=0) - onehot) * onehot, axis=1)
    replica = row_rank % replicas
    slot_place = row_rank // replicas
    slot_id = replica * EXPERTS + flat_expert
    holder = slot_id // slots_dev
    local_slot = slot_id % slots_dev
    buffer_spot = (local_slot * groups + holder) * capacity + slot_place
    buffer_rows = slots_dev * groups * capacity
    send_table = (
        jnp.full((buffer_rows,), flat_count, jnp.int32)
        .at[buffer_spot]
        .set(jnp.arange(flat_count, dtype=jnp.int32))
    )
    token_index = send_table // top_count
    source = jnp.concatenate([mixed_rows, jnp.zeros((1, quarter), jnp.bfloat16)], axis=0)
    outgoing = source[token_index].reshape(slots_dev, groups, capacity, quarter)
    arrived = lax.all_to_all(outgoing, "ep", split_axis=1, concat_axis=1, tiled=True)
    rows_in = arrived.reshape(slots_dev, groups * capacity, quarter)
    full_rows = lax.all_gather(rows_in, "hid", axis=2, tiled=True)
    gate_cols = gate_up.reshape(slots_dev, full_width, 2 * group_width)
    hidden = expert_hidden(full_rows, gate_cols, group_width)
    partial_value = jnp.einsum(
        "jrf,jfd->jrd", hidden, down_proj, preferred_element_type=jnp.float32
    )
    result = lax.psum_scatter(
        partial_value.astype(jnp.bfloat16), "hid", scatter_dimension=2, tiled=True
    )
    returned = lax.all_to_all(
        result.reshape(slots_dev, groups, capacity, quarter),
        "ep",
        split_axis=1,
        concat_axis=1,
        tiled=True,
    )
    flat_output = returned.reshape(buffer_rows, quarter)
    picked = flat_output[buffer_spot].reshape(tok_rows, top_count, quarter).astype(jnp.float32)
    mixture = jnp.sum(picked * route_weight[:, :, None], axis=1)
    residual = mixed_rows.astype(jnp.float32) + mixture
    squares = lax.psum(jnp.sum(residual * residual, axis=1), "hid")
    inverse_rms = lax.rsqrt(squares / full_width + epsilon)
    normed = (residual * inverse_rms[:, None] * norm_gain[None, :]).astype(jnp.bfloat16)
    return (residual.astype(jnp.bfloat16), normed)


def solution(mesh):
    in_specs = (
        P("ep", "hid"),
        P("ep", "hid"),
        P("hid", None),
        P("ep", None),
        P("ep", None),
        P("ep", None, None, "hid"),
        P("ep", "hid", None),
        P("hid"),
    )
    out_specs = (P("ep", "hid"), P("ep", "hid"))
    return jax.shard_map(
        on_device, mesh=mesh, in_specs=in_specs, out_specs=out_specs, check_vma=False
    )
```

profile of v0, /device:TPU:1, one launch (start us, length us, event | category | flops | bytes accessed | tf_op | source)
XLA Modules:
  0.0 194.6 jit_solution(5431213657208205530)
XLA Ops:
  7.2 0.0 copy-start
  7.2 0.0 copy-start.4
  7.2 0.0 copy-start.2
  7.2 0.0 reduce-scatter.7.cloned.1.call-start
  7.2 1.7 convolution_convert_fusion.1
  9.0 0.9 copy.23
  9.9 0.0 reduce-scatter.7.cloned.1.call-update
  9.9 0.0 all-gather.2.cloned.1.call-start
  9.9 0.0 copy-done.4
  10.0 0.1 copy.16
  10.1 0.1 eq.32
  10.2 0.1 eq.28
  10.3 0.1 reshape.157
  10.4 0.6 reduce-window.6
  11.0 0.2 slice_reduce_fusion
  11.2 0.1 fusion.14
  11.4 1.4 scatter_custom_fusion
  12.8 27.7 %reduce-scatter.7.cloned.1.call-done = bf16[384,64]{1,0:T(8,128)(2,1)} async-done(((bf16[1536,64]{1,0:T(8,128)(2,1)}), bf16[384,64]{1,0:T(8,128)(2,1)}) %reduce-scatter.7.cloned.1.call-update) | async-done | bytes 49168
  40.5 1.0 copy.24
  41.5 0.0 copy-done.2
  41.5 1.9 gather_fusion
  43.5 0.1 reshape.158
  43.6 32.9 %all_to_all.10 = bf16[1,128,4,384]{3,2,0,1:T(4,128)(2,1)S(1)} all-to-all(bf16[1,128,4,384]{3,2,0,1:T(4,128)(2,1)S(1)} %bitcast.58), channel_id=1, replica_groups=mesh['ep'=128,'hid'=4] {'ep'}, dimensions={1} | all-to-all | bytes 786432 | tf_op jit(solution)/shard_map/all_to_all | solution.py:54
  76.5 0.8 reshape.159
  77.4 0.0 all-gather.2.cloned.1.call-update
  77.4 0.0 reduce-scatter.9.cloned.1.call-start
  77.4 23.8 %all-gather.2.cloned.1.call-done = bf16[1,512,1536]{2,1,0:T(8,128)(2,1)} async-done(((bf16[1,512,384]{2,1,0:T(8,128)(2,1)}), bf16[1,512,1536]{2,1,0:T(8,128)(2,1)}) %all-gather.2.cloned.1.call-update) | async-done | bytes 1572880 | tf_op jit(solution)/shard_map/all_gather | solution.py:56
  101.3 0.0 copy-done
  101.3 0.0 copy-start.1
  101.3 2.3 %fusion.3 = f32[1,512,384]{1,2,0:T(8,128)S(1)} fusion(bf16[1536,384]{0,1:T(8,128)(2,1)S(1)} %bitcast.54, bf16[1,512,1536]{2,1,0:T(8,128)(2,1)} %all-gather.2.cloned.1.call-done), kind=kOutput, calls=%fused_computation.9 | convolution fusion | flops 603979776 | bytes 3538944 | tf_op jit(solution)/shard_map/jrd,jdf->jrf/dot_general | solution.py:14
  103.5 0.0 copy-done.1
  103.6 0.6 fusion
  104.2 5.7 %copy.25 = bf16[1,512,1536]{1,0,2:T(2,128)(2,1)} copy(bf16[1,512,1536]{2,1,0:T(8,128)(2,1)S(1)} %fusion) | data formatting | bytes 3145728
  109.8 3.5 %copy.31 = bf16[1536,1,512]{2,0,1:T(8,128)(2,1)} copy(bf16[1536,1,512]{2,1,0:T(2,128)(2,1)} %bitcast.55) | data formatting | bytes 3145728
  113.3 0.0 reduce-scatter.9.cloned.1.call-update
  113.3 30.3 %reduce-scatter.9.cloned.1.call-done = bf16[384,512]{1,0:T(8,128)(2,1)} async-done(((bf16[1536,512]{1,0:T(8,128)(2,1)}), bf16[384,512]{1,0:T(8,128)(2,1)}) %reduce-scatter.9.cloned.1.call-update) | async-done | bytes 393232
  143.6 1.4 reshape_bitcast_fusion
  145.0 0.0 copy-start.5
  145.0 0.6 copy.26
  145.6 0.8 reshape.164
  146.4 15.3 %all-to-all-start.1 = ((bf16[1,128,4,384]{3,2,0,1:T(4,128)(2,1)}), bf16[1,128,4,384]{3,2,0,1:T(4,128)(2,1)S(1)}, u32[]{:S(2)}, u32[]{:S(2)}) async-start(bf16[1,128,4,384]{3,2,0,1:T(4,128)(2,1)} %bitcast.10), calls=%async_computation.1 | async-start | bytes 786432 | tf_op jit(solution)/shard_map/all_to_all | solution.py:65
  161.7 0.0 copy-done.5
  161.7 0.1 copy.22
  161.8 16.7 %all-to-all-done.1 = bf16[1,128,4,384]{3,2,0,1:T(4,128)(2,1)S(1)} async-done(((bf16[1,128,4,384]{3,2,0,1:T(4,128)(2,1)}), bf16[1,128,4,384]{3,2,0,1:T(4,128)(2,1)S(1)}, u32[]{:S(2)}, u32[]{:S(2)}) %all-to-all-start.1) | async-done | bytes 393248 | tf_op jit(solution)/shard_map/all_to_all | solution.py:65
  178.5 0.1 reshape.165
  178.6 0.0 copy-start.3
  178.6 1.2 gather_fusion.1
  179.8 0.1 reshape.166
  179.9 0.3 multiply_reduce_fusion
  180.2 0.1 multiply_reduce_fusion.1
  180.3 7.0 %psum.7 = f32[64]{0:T(128)S(1)} all-reduce(f32[64]{0:T(128)S(1)} %multiply_reduce_fusion.1), channel_id=1, replica_groups=mesh['ep'=128,'hid'=4] {'hid'}, use_global_device_ids=true, to_apply=%region_8.9 | all-reduce | flops 64 | bytes 512 | tf_op jit(solution)/shard_map/psum | solution.py:76
  187.4 0.0 copy-done.3
  187.4 0.7 multiply_convert_fusion
  (11 shorter events, 0.1 us)
Async XLA Ops:
  7.2 94.1 %copy-start = (bf16[1,1536,2,192]{1,3,2,0:T(8,128)(2,1)S(1)}, bf16[1,1536,2,192]{1,3,2,0:T(8,128)(2,1)}, u32[]{:S(2)}) copy-start(bf16[1,1536,2,192]{1,3,2,0:T(8,128)(2,1)} %param.13) | copy-start | bytes 3538948
  7.2 2.8 %copy-start.4 = (s32[64,4]{0,1:T(4,128)S(1)}, s32[64,4]{0,1:T(4,128)}, u32[]{:S(2)}) copy-start(s32[64,4]{0,1:T(4,128)} %param.11) | copy-start | bytes 3076
  7.2 34.3 %copy-start.2 = (bf16[64,384]{1,0:T(8,128)(2,1)S(1)}, bf16[64,384]{1,0:T(8,128)(2,1)}, u32[]{:S(2)}) copy-start(bf16[64,384]{1,0:T(8,128)(2,1)} %param.9) | copy-start | bytes 147460
  7.2 33.3 %reduce-scatter.7.cloned.1.call-start = ((), (), s32[]{:S(2)}) async-start(), calls=%async_computation.5 | async-start | bytes 491520
  9.9 91.4 %all-gather.2.cloned.1.call-start = ((), (), s32[]{:S(2)}) async-start(), calls=%async_computation.4 | async-start | bytes 1966080 | tf_op jit(solution)/shard_map/all_gather | solution.py:56
  77.4 66.2 %reduce-scatter.9.cloned.1.call-start = ((), (), s32[]{:S(2)}) async-start(), calls=%async_computation.6 | async-start | bytes 1966080
  101.3 2.3 %copy-start.1 = (bf16[1,192,1536]{2,1,0:T(8,128)(2,1)S(1)}, bf16[1,192,1536]{2,1,0:T(8,128)(2,1)}, u32[]{:S(2)}) copy-start(bf16[1,192,1536]{2,1,0:T(8,128)(2,1)} %param.14) | copy-start | bytes 1769476
  145.0 16.7 %copy-start.5 = (f32[64,4]{0,1:T(4,128)S(1)}, f32[64,4]{0,1:T(4,128)}, u32[]{:S(2)}) copy-start(f32[64,4]{0,1:T(4,128)} %param.12) | copy-start | bytes 3076
  146.4 32.1 %all-to-all-start.1 = ((bf16[1,128,4,384]{3,2,0,1:T(4,128)(2,1)}), bf16[1,128,4,384]{3,2,0,1:T(4,128)(2,1)S(1)}, u32[]{:S(2)}, u32[]{:S(2)}) async-start(bf16[1,128,4,384]{3,2,0,1:T(4,128)(2,1)} %bitcast.10), calls=%async_computation.1 | async-start | bytes 786432 | tf_op jit(solution)/shard_map/all_to_all | solution.py:65
  178.6 8.8 %copy-start.3 = (f32[384]{0:T(512)S(1)}, f32[384]{0:T(512)}, u32[]{:S(2)}) copy-start(f32[384]{0:T(512)} %param.15) | copy-start | bytes 4612
Sparse Core Ops, SparseCore 0:
  10.9 29.5 reduce-scatter.6
  77.5 23.7 all-gather.1
  113.4 30.1 reduce-scatter.8
where the time goes:
time: 197 us; the launch traced here: 195 us
  waiting for transfers between devices  98.6 us (50%)
  blocking collectives  40 us (20%)
  local copies, waits for them, and re-layouts  20.2 us (10%)
  starting transfers between devices  15.4 us (8%)
  between operations  14 us (7%)
  matrix products  4.59 us (2%)
    unnamed x5, waiting for transfers between devices  58 us
    all_to_all x1, blocking collectives, on_device(): lax.all_to_all(outgoing, 'ep', split_axis=1, concat_axis=1, tiled=True)  32.9 us
    all_gather x1, waiting for transfers between devices, on_device(): full_rows = lax.all_gather(rows_in, 'hid', axis=2, tiled=True)  23.8 us
    all_to_all x1, waiting for transfers between devices, on_device(): lax.all_to_all(result.reshape(slots_dev, groups, capacity, quarter), 'ep'...  16.7 us
    all_to_all x1, starting transfers between devices, on_device(): lax.all_to_all(result.reshape(slots_dev, groups, capacity, quarter), 'ep'...  15.3 us
    unnamed x20, local copies, waits for them, and re-layouts  13.2 us
    psum x1, blocking collectives, on_device(): squares = lax.psum(jnp.sum(residual * residual, axis=1), 'hid')  7.04 us
  transfers between devices with their start and end apart: 4, of which 4 were waited for; matrix products, arithmetic and copies ran while one was open for 1% of the time, Pallas kernels for 0%

commit v1 on v0

v1 whole, which is shorter than its diff:
```python
import functools

import jax
import jax.numpy as jnp
from jax import lax
from jax.experimental import pallas as pl
from jax.experimental.pallas import tpu as pltpu
from jax.sharding import PartitionSpec as P

EXPERTS = 32
MOST = 16
HID = 4
CHUNKS = 4
EPSILON = 1e-06
BF = jnp.bfloat16
F32 = jnp.float32


def dot(a, b):
    return jnp.dot(a, b, preferred_element_type=F32)


def kernel(
    att_ref, stream_ref, routes_ref, rw_ref, gain_ref, ow_hbm, gate_hbm, up_hbm, down_hbm,
    sout_ref, normed_ref,
    ow_v, gate_v, up_v, down_v, proj, projr, outg, full, part, partr, res, ret, sq,
    w_sem, p_send, p_recv, d_send, d_recv, f_send, f_recv, s_send, s_recv, r_send, r_recv,
    q_send, q_recv,
):
    me = lax.axis_index("ep")
    hid = lax.axis_index("hid")
    loc = lax.rem(me, EXPERTS)
    base = me - loc
    tok, quarter = stream_ref.shape
    rows = EXPERTS * MOST
    shifts = EXPERTS // CHUNKS
    crows = rows // CHUNKS

    def ahead(i):
        return base + lax.rem(loc + i, EXPERTS)

    def behind(i):
        return base + lax.rem(loc + EXPERTS - i, EXPERTS)

    def hid_up(j):
        return lax.rem(hid + j, HID)

    def cols(j):
        return pl.ds(pl.multiple_of(hid_up(j) * quarter, quarter), quarter)

    def slot(i):
        return pl.ds(pl.multiple_of(i * MOST, MOST), MOST)

    def chunk(c):
        return pl.ds(c * crows, crows)

    loads = [
        pltpu.make_async_copy(src, dst, w_sem.at[n])
        for n, (src, dst) in enumerate(
            [(ow_hbm, ow_v), (gate_hbm, gate_v), (up_hbm, up_v), (down_hbm, down_v)]
        )
    ]
    for load in loads:
        load.start()

    barrier = pltpu.get_barrier_semaphore()

    def greet(i, carry):
        pl.semaphore_signal(
            barrier, inc=1, device_id={"ep": ahead(i), "hid": hid},
            device_id_type=pl.DeviceIdType.MESH,
        )
        return carry

    lax.fori_loop(1, EXPERTS, greet, 0)
    for j in range(1, HID):
        pl.semaphore_signal(
            barrier, inc=1, device_id={"ep": me, "hid": hid_up(j)},
            device_id_type=pl.DeviceIdType.MESH,
        )

    def over_hid(src, dst, send, recv, j):
        return pltpu.make_async_remote_copy(
            src_ref=src, dst_ref=dst, send_sem=send, recv_sem=recv,
            device_id={"ep": me, "hid": hid_up(j)}, device_id_type=pl.DeviceIdType.MESH,
        )

    def p_copy(j):
        return over_hid(proj.at[j], projr.at[j], p_send.at[j], p_recv.at[j], j)

    def f_copy(j, c):
        return pltpu.make_async_remote_copy(
            src_ref=full.at[0, chunk(c)], dst_ref=full.at[j, chunk(c)],
            send_sem=f_send.at[j, c], recv_sem=f_recv.at[j, c],
            device_id={"ep": me, "hid": hid_up(HID - j)}, device_id_type=pl.DeviceIdType.MESH,
        )

    def s_copy(j, c):
        return over_hid(
            part.at[j, chunk(c)], partr.at[j, chunk(c)], s_send.at[j, c], s_recv.at[j, c], j
        )

    def q_copy(j):
        return over_hid(sq.at[0], sq.at[j], q_send.at[j], q_recv.at[j], j)

    def d_copy(i):
        return pltpu.make_async_remote_copy(
            src_ref=outg.at[slot(i)], dst_ref=full.at[0, slot(i)],
            send_sem=d_send.at[i], recv_sem=d_recv.at[i],
            device_id={"ep": ahead(i), "hid": hid}, device_id_type=pl.DeviceIdType.MESH,
        )

    def r_copy(i):
        return pltpu.make_async_remote_copy(
            src_ref=res.at[slot(i)], dst_ref=ret.at[slot(i)],
            send_sem=r_send.at[i], recv_sem=r_recv.at[i],
            device_id={"ep": behind(i), "hid": hid}, device_id_type=pl.DeviceIdType.MESH,
        )

    def each(low, high, act):
        def body(i, carry):
            act(i)
            return carry

        lax.fori_loop(low, high, body, 0)

    def span(c):
        return max(1, c * shifts), (c + 1) * shifts

    att = att_ref[...]
    loads[0].wait()
    for j in range(HID):
        proj[j] = dot(att, ow_v[:, cols(j)]).astype(BF)
    pl.semaphore_wait(barrier, EXPERTS - 1 + HID - 1)
    for j in (2, 1, 3):
        p_copy(j).start()

    column = lax.broadcasted_iota(jnp.int32, (tok, rows), 1)
    expert = (loc + column // MOST) % EXPERTS
    place = (column % MOST).astype(F32)
    named = jnp.zeros((tok, rows), F32)
    weight = jnp.zeros((tok, rows), F32)
    for k in range(routes_ref.shape[1]):
        same = routes_ref[:, k : k + 1] == expert
        named = named + jnp.where(same, 1.0, 0.0)
        weight = weight + jnp.where(same, rw_ref[:, k : k + 1], 0.0)
    earlier = jnp.where(
        lax.broadcasted_iota(jnp.int32, (tok, tok), 1)
        < lax.broadcasted_iota(jnp.int32, (tok, tok), 0),
        1.0,
        0.0,
    ).astype(BF)
    rank = dot(earlier, named.astype(BF))
    hit = jnp.where(rank == place, named, 0.0)
    pick = hit.astype(BF).T
    scaled = hit * weight
    high = scaled.astype(BF)
    low = (scaled - high.astype(F32)).astype(BF)

    total = proj[0].astype(F32)
    for j in range(1, HID):
        p_copy(j).wait_recv()
        total = total + projr[j].astype(F32)
    mixed = (stream_ref[...].astype(F32) + total.astype(BF).astype(F32)).astype(BF)

    for c in range(CHUNKS):
        block = dot(pick[c * crows : (c + 1) * crows], mixed).astype(BF)
        outg[chunk(c)] = block
        if c == 0:
            full[0, 0:MOST] = block[0:MOST]
        each(*span(c), lambda i: d_copy(i).start())

    def gather(c):
        each(*span(c), lambda i: d_copy(i).wait_recv())
        for j in (2, 1, 3):
            f_copy(j, c).start()

    def compute(c):
        gate = jnp.zeros((crows, gate_v.shape[1]), F32)
        up = jnp.zeros((crows, gate_v.shape[1]), F32)
        for j in (0, 1, 3, 2):
            if j:
                f_copy(j, c).wait_recv()
            features = full[j, chunk(c)]
            gate = gate + dot(features, gate_v[cols(j), :])
            up = up + dot(features, up_v[cols(j), :])
        hidden = (jnp.maximum(gate, 0.0) * up).astype(BF)
        for j in (2, 1, 3, 0):
            part[j, chunk(c)] = dot(hidden, down_v[:, cols(j)]).astype(BF)
            if j:
                s_copy(j, c).start()

    def give_back(c):
        value = part[0, chunk(c)].astype(F32)
        for j in range(1, HID):
            s_copy(j, c).wait_recv()
            value = value + partr[j, chunk(c)].astype(F32)
        value = value.astype(BF)
        res[chunk(c)] = value
        if c == 0:
            ret[0:MOST] = value[0:MOST]
        each(*span(c), lambda i: r_copy(i).start())

    gather(0)
    gather(1)
    for n in range(1, 4):
        loads[n].wait()
    compute(0)
    gather(2)
    compute(1)
    gather(3)
    give_back(0)
    compute(2)
    give_back(1)
    compute(3)
    give_back(2)
    give_back(3)

    mixture = jnp.zeros((tok, quarter), F32)
    for c in range(CHUNKS):
        each(*span(c), lambda i: r_copy(i).wait_recv())
        back = ret[chunk(c)]
        mixture = mixture + dot(high[:, c * crows : (c + 1) * crows], back)
        mixture = mixture + dot(low[:, c * crows : (c + 1) * crows], back)
    residual = mixed.astype(F32) + mixture
    sout_ref[...] = residual.astype(BF)
    squares = residual * residual
    lanes = squares[:, 0:128]
    for n in range(1, quarter // 128):
        lanes = lanes + squares[:, n * 128 : (n + 1) * 128]
    sq[0] = lanes
    for j in (2, 1, 3):
        q_copy(j).start()

    for j in range(1, HID):
        p_copy(j).wait_send()
        for c in range(CHUNKS):
            f_copy(j, c).wait_send()
            s_copy(j, c).wait_send()
    each(1, EXPERTS, lambda i: d_copy(i).wait_send())
    each(1, EXPERTS, lambda i: r_copy(i).wait_send())

    for j in range(1, HID):
        q_copy(j).wait_recv()
        lanes = lanes + sq[j]
    rms = jnp.sum(lanes, axis=1, keepdims=True) / (quarter * HID)
    normed_ref[...] = (residual * lax.rsqrt(rms + EPSILON) * gain_ref[...]).astype(BF)
    for j in range(1, HID):
        q_copy(j).wait_send()


def on_device(attention, stream, o_weight, routes, route_weight, gate_up, down_proj, norm_gain):
    tok, quarter = stream.shape
    full_width = quarter * HID
    width = gate_up.shape[3]
    rows = EXPERTS * MOST
    gate = gate_up[0, :, 0, :]
    up = gate_up[0, :, 1, :]
    down = down_proj[0]
    vmem = pl.BlockSpec(memory_space=pltpu.VMEM)
    hbm = pl.BlockSpec(memory_space=pl.ANY)
    dma = pltpu.SemaphoreType.DMA
    return pl.pallas_call(
        kernel,
        out_shape=(
            jax.ShapeDtypeStruct((tok, quarter), BF),
            jax.ShapeDtypeStruct((tok, quarter), BF),
        ),
        in_specs=[vmem] * 5 + [hbm] * 4,
        out_specs=(vmem, vmem),
        scratch_shapes=[
            pltpu.VMEM(o_weight.shape, BF),
            pltpu.VMEM(gate.shape, BF),
            pltpu.VMEM(up.shape, BF),
            pltpu.VMEM(down.shape, BF),
            pltpu.VMEM((HID, tok, quarter), BF),
            pltpu.VMEM((HID, tok, quarter), BF),
            pltpu.VMEM((rows, quarter), BF),
            pltpu.VMEM((HID, rows, quarter), BF),
            pltpu.VMEM((HID, rows, quarter), BF),
            pltpu.VMEM((HID, rows, quarter), BF),
            pltpu.VMEM((rows, quarter), BF),
            pltpu.VMEM((rows, quarter), BF),
            pltpu.VMEM((HID, tok, 128), F32),
            dma((4,)),
            dma((HID,)), dma((HID,)),
            dma((EXPERTS,)), dma((EXPERTS,)),
            dma((HID, CHUNKS)), dma((HID, CHUNKS)),
            dma((HID, CHUNKS)), dma((HID, CHUNKS)),
            dma((EXPERTS,)), dma((EXPERTS,)),
            dma((HID,)), dma((HID,)),
        ],
        compiler_params=pltpu.CompilerParams(collective_id=0, has_side_effects=True),
    )(
        attention, stream, routes, route_weight, norm_gain.reshape(1, quarter),
        o_weight, gate, up, down,
    )


def solution(mesh):
    in_specs = (
        P("ep", "hid"),
        P("ep", "hid"),
        P("hid", None),
        P("ep", None),
        P("ep", None),
        P("ep", None, None, "hid"),
        P("ep", "hid", None),
        P("hid"),
    )
    out_specs = (P("ep", "hid"), P("ep", "hid"))
    return jax.shard_map(
        on_device, mesh=mesh, in_specs=in_specs, out_specs=out_specs, check_vma=False
    )
```

time: 197 us -> 87.3 us (0.44)
  waiting for transfers between devices: 98.6 us -> 0 us
  Pallas kernels: 0 us -> 77.5 us
  blocking collectives: 40 us -> 0 us
  starting transfers between devices: 15.4 us -> 0 us
  between operations: 14 us -> 0.67 us
  local copies, waits for them, and re-layouts: 20.2 us -> 8.52 us
  matrix products: 4.59 us -> 0 us
    pallas_call x0 -> x1, Pallas kernels: none -> 77.5 us  [on_device(): pl.pallas_call(kernel, out_shape=(jax.ShapeDtypeStruct((tok, quarter), BF...]
    unnamed x5 -> x0, waiting for transfers between devices: 58 us -> none
    all_to_all x1 -> x0, blocking collectives: 32.9 us -> none  [on_device(): lax.all_to_all(outgoing, 'ep', split_axis=1, concat_axis=1, tiled=True)]
    all_gather x1 -> x0, waiting for transfers between devices: 23.8 us -> none  [on_device(): full_rows = lax.all_gather(rows_in, 'hid', axis=2, tiled=True)]
    all_to_all x1 -> x0, waiting for transfers between devices: 16.7 us -> none  [on_device(): lax.all_to_all(result.reshape(slots_dev, groups, capacity, quarter), 'ep'...]
    all_to_all x1 -> x0, starting transfers between devices: 15.3 us -> none  [on_device(): lax.all_to_all(result.reshape(slots_dev, groups, capacity, quarter), 'ep'...]
    psum x1 -> x0, blocking collectives: 7.04 us -> none  [on_device(): squares = lax.psum(jnp.sum(residual * residual, axis=1), 'hid')]
    unnamed x20 -> x12, local copies, waits for them, and re-layouts: 13.2 us -> 6.62 us
  transfers between devices with their start and end apart: 4 -> 0, of which waited for: 4 -> 0; matrix products, arithmetic and copies ran while one was open for 1% -> 0% of each run, Pallas kernels for 0% -> 0%
where the time goes in v1:
time: 87.3 us; the launch traced here: 86.7 us
  Pallas kernels  77.5 us (89%)
  local copies, waits for them, and re-layouts  8.52 us (10%)
    pallas_call x1, Pallas kernels, on_device(): pl.pallas_call(kernel, out_shape=(jax.ShapeDtypeStruct((tok, quarter), BF...  77.5 us
    unnamed x12, local copies, waits for them, and re-layouts  6.62 us

profile of v1, /device:TPU:1, one launch (start us, length us, event | category | flops | bytes accessed | tf_op | source)
XLA Modules:
  0.0 86.7 jit_solution(18081501189020755255)
XLA Ops:
  0.6 1.3 %fusion = (bf16[1,1536,1,192]{1,3,2,0:T(8,128)(2,1)S(1)}, bf16[1,1536,1,192]{1,3,2,0:T(8,128)(2,1)S(1)}) fusion(bf16[1,1536,2,192]{1,3,2,0:T(8,128)(2,1)} %param.13), kind=kLoop, calls=%fused_computation | loop fusion | bytes 2359296 | tf_op jit(solution)/shard_map/slice | solution.py:258
  2.0 0.0 copy-start
  2.0 0.0 copy-start.1
  2.0 0.0 copy-start.2
  2.0 1.2 %copy.14 = bf16[1,1536,1,192]{3,1,2,0:T(8,128)(2,1)} copy(bf16[1,1536,1,192]{1,3,2,0:T(8,128)(2,1)S(1)} %get-tuple-element.3) | data formatting | bytes 1179648
  3.2 1.2 %copy.15 = bf16[1,1536,1,192]{3,1,2,0:T(8,128)(2,1)} copy(bf16[1,1536,1,192]{1,3,2,0:T(8,128)(2,1)S(1)} %get-tuple-element.2) | data formatting | bytes 1179648
  4.3 0.0 copy-done
  4.3 0.7 copy.12.routes_ref
  5.0 0.0 copy-done.1
  5.0 0.7 copy.13.rw_ref
  5.7 0.0 copy-done.2
  5.8 0.6 reshape.7.gain_ref
  6.3 77.5 %shard_map.95 = (bf16[64,384]{1,0:T(8,128)(2,1)}, bf16[64,384]{1,0:T(8,128)(2,1)}) custom-call(bf16[64,384]{1,0:T(8,128)(2,1)} %att_ref.1, bf16[64,384]{1,0:T(8,128)(2,1)} %stream_ref.1, s32[64,4]{1,0:T(8,128)} %copy.12.routes_ref, f32[64,4]{1,0:T(8,128)} %copy.13.rw_ref, f32[1,384]{1,0:T(1,128)} %reshape.7.gain_ref, bf16[384,1536]{1,0:T(8,128)(2,1)} %ow_hbm.1, ...), custom_call_target="tpu_custom_call" | custom-call | tf_op jit(solution)/shard_map/pallas_call | solution.py:263
  83.8 1.4 %copy.18 = bf16[64,384]{1,0:T(8,128)(2,1)} copy(bf16[64,384]{1,0:T(8,128)(2,1)} %get-tuple-element.6) | data formatting | bytes 98304
  85.2 1.4 %copy.19 = bf16[64,384]{1,0:T(8,128)(2,1)} copy(bf16[64,384]{1,0:T(8,128)(2,1)} %get-tuple-element.7) | data formatting | bytes 98304
Async XLA Ops:
  2.0 2.4 %copy-start = (s32[64,4]{0,1:T(4,128)S(1)}, s32[64,4]{0,1:T(4,128)}, u32[]{:S(2)}) copy-start(s32[64,4]{0,1:T(4,128)} %param.11) | copy-start | bytes 3076
  2.0 3.1 %copy-start.1 = (f32[64,4]{0,1:T(4,128)S(1)}, f32[64,4]{0,1:T(4,128)}, u32[]{:S(2)}) copy-start(f32[64,4]{0,1:T(4,128)} %param.12) | copy-start | bytes 3076
  2.0 3.8 %copy-start.2 = (f32[384]{0:T(512)S(1)}, f32[384]{0:T(512)}, u32[]{:S(2)}) copy-start(f32[384]{0:T(512)} %param.15) | copy-start | bytes 4612

commit v2 on v1

--- a/solution.py
+++ b/solution.py
@@ -1,5 +1,3 @@
-import functools
-
 import jax
 import jax.numpy as jnp
 from jax import lax
@@ -20,10 +18,14 @@
     return jnp.dot(a, b, preferred_element_type=F32)
 
 
+def dot_t(a, b):
+    return lax.dot_general(a, b, (((1,), (1,)), ((), ())), preferred_element_type=F32)
+
+
 def kernel(
-    att_ref, stream_ref, routes_ref, rw_ref, gain_ref, ow_hbm, gate_hbm, up_hbm, down_hbm,
-    sout_ref, normed_ref,
-    ow_v, gate_v, up_v, down_v, proj, projr, outg, full, part, partr, res, ret, sq,
+    att_ref, stream_ref, routes_ref, rw_ref, ow_hbm, gu_hbm, down_hbm,
+    residual_ref, scaled_ref,
+    ow_v, gu_v, down_v, proj, projr, outg, full, part, partr, passing, res, ret, sq,
     w_sem, p_send, p_recv, d_send, d_recv, f_send, f_recv, s_send, s_recv, r_send, r_recv,
     q_send, q_recv,
 ):
@@ -35,6 +37,8 @@
     rows = EXPERTS * MOST
     shifts = EXPERTS // CHUNKS
     crows = rows // CHUNKS
+    hrows = crows // 2
+    width = gu_v.shape[0] // 2
 
     def ahead(i):
         return base + lax.rem(loc + i, EXPERTS)
@@ -53,11 +57,14 @@
 
     def chunk(c):
         return pl.ds(c * crows, crows)
+
+    def half(c, b):
+        return pl.ds(c * crows + b * hrows, hrows)
 
     loads = [
         pltpu.make_async_copy(src, dst, w_sem.at[n])
         for n, (src, dst) in enumerate(
-            [(ow_hbm, ow_v), (gate_hbm, gate_v), (up_hbm, up_v), (down_hbm, down_v)]
+            [(ow_hbm, ow_v), (gu_hbm, gu_v), (down_hbm, down_v)]
         )
     ]
     for load in loads:
@@ -95,9 +102,24 @@
             device_id={"ep": me, "hid": hid_up(HID - j)}, device_id_type=pl.DeviceIdType.MESH,
         )
 
-    def s_copy(j, c):
+    def f_pass(b, c):
+        j = 1 + 2 * b
+        return pltpu.make_async_remote_copy(
+            src_ref=full.at[j, half(c, b)], dst_ref=full.at[2, half(c, b)],
+            send_sem=f_send.at[2 * b, c], recv_sem=f_recv.at[2 * b, c],
+            device_id={"ep": me, "hid": hid_up(HID - j)}, device_id_type=pl.DeviceIdType.MESH,
+        )
+
+    def s_copy(j, b, c):
         return over_hid(
-            part.at[j, chunk(c)], partr.at[j, chunk(c)], s_send.at[j, c], s_recv.at[j, c], j
+            part.at[j, half(c, b)], partr.at[j // 2, half(c, b)],
+            s_send.at[j // 2, b, c], s_recv.at[j // 2, b, c], j
+        )
+
+    def s_pass(b, c):
+        return over_hid(
+            part.at[2, half(c, b)], passing.at[half(c, b)],
+            s_send.at[2, b, c], s_recv.at[2, b, c], 1 + 2 * b
         )
 
     def q_copy(j):
@@ -135,25 +157,25 @@
     for j in (2, 1, 3):
         p_copy(j).start()
 
-    column = lax.broadcasted_iota(jnp.int32, (tok, rows), 1)
-    expert = (loc + column // MOST) % EXPERTS
-    place = (column % MOST).astype(F32)
-    named = jnp.zeros((tok, rows), F32)
-    weight = jnp.zeros((tok, rows), F32)
-    for k in range(routes_ref.shape[1]):
-        same = routes_ref[:, k : k + 1] == expert
+    row = lax.broadcasted_iota(jnp.int32, (rows, tok), 0)
+    expert = (loc + row // MOST) % EXPERTS
+    place = (row % MOST).astype(F32)
+    named = jnp.zeros((rows, tok), F32)
+    weight = jnp.zeros((rows, tok), F32)
+    for k in range(routes_ref.shape[0]):
+        same = routes_ref[k : k + 1, :] == expert
         named = named + jnp.where(same, 1.0, 0.0)
-        weight = weight + jnp.where(same, rw_ref[:, k : k + 1], 0.0)
+        weight = weight + jnp.where(same, rw_ref[k : k + 1, :], 0.0)
     earlier = jnp.where(
-        lax.broadcasted_iota(jnp.int32, (tok, tok), 1)
-        < lax.broadcasted_iota(jnp.int32, (tok, tok), 0),
+        lax.broadcasted_iota(jnp.int32, (tok, tok), 0)
+        < lax.broadcasted_iota(jnp.int32, (tok, tok), 1),
         1.0,
         0.0,
     ).astype(BF)
-    rank = dot(earlier, named.astype(BF))
+    rank = dot(named.astype(BF), earlier)
     hit = jnp.where(rank == place, named, 0.0)
-    pick = hit.astype(BF).T
-    scaled = hit * weight
+    pick = hit.astype(BF)
+    scaled = (hit * weight).T
     high = scaled.astype(BF)
     low = (scaled - high.astype(F32)).astype(BF)
 
@@ -172,30 +194,47 @@
 
     def gather(c):
         each(*span(c), lambda i: d_copy(i).wait_recv())
-        for j in (2, 1, 3):
+        for j in (1, 3):
             f_copy(j, c).start()
 
+    def gather_on(c):
+        for b in range(2):
+            f_copy(1 + 2 * b, c).wait_recv()
+            f_pass(b, c).start()
+
     def compute(c):
-        gate = jnp.zeros((crows, gate_v.shape[1]), F32)
-        up = jnp.zeros((crows, gate_v.shape[1]), F32)
+        gate = jnp.zeros((crows, width), F32)
+        up = jnp.zeros((crows, width), F32)
         for j in (0, 1, 3, 2):
-            if j:
-                f_copy(j, c).wait_recv()
+            if j == 2:
+                f_pass(0, c).wait_recv()
+                f_pass(1, c).wait_recv()
             features = full[j, chunk(c)]
-            gate = gate + dot(features, gate_v[cols(j), :])
-            up = up + dot(features, up_v[cols(j), :])
+            gate = gate + dot_t(features, gu_v[:width, cols(j)])
+            up = up + dot_t(features, gu_v[width:, cols(j)])
         hidden = (jnp.maximum(gate, 0.0) * up).astype(BF)
-        for j in (2, 1, 3, 0):
+        part[2, chunk(c)] = dot(hidden, down_v[:, cols(2)]).astype(BF)
+        for b in range(2):
+            s_pass(b, c).start()
+        for j in (1, 3):
             part[j, chunk(c)] = dot(hidden, down_v[:, cols(j)]).astype(BF)
-            if j:
-                s_copy(j, c).start()
+            s_copy(j, (3 - j) // 2, c).start()
+        part[0, chunk(c)] = dot(hidden, down_v[:, cols(0)]).astype(BF)
+
+    def sum_on(c):
+        for b in range(2):
+            j = 1 + 2 * b
+            s_pass(b, c).wait_recv()
+            both = part[j, half(c, b)].astype(F32) + passing[half(c, b)].astype(F32)
+            part[j, half(c, b)] = both.astype(BF)
+            s_copy(j, b, c).start()
 
     def give_back(c):
-        value = part[0, chunk(c)].astype(F32)
-        for j in range(1, HID):
-            s_copy(j, c).wait_recv()
-            value = value + partr[j, chunk(c)].astype(F32)
-        value = value.astype(BF)
+        for j in (1, 3):
+            for b in range(2):
+                s_copy(j, b, c).wait_recv()
+        value = part[0, chunk(c)].astype(F32) + partr[0, chunk(c)].astype(F32)
+        value = (value + partr[1, chunk(c)].astype(F32)).astype(BF)
         res[chunk(c)] = value
         if c == 0:
             ret[0:MOST] = value[0:MOST]
@@ -203,16 +242,24 @@
 
     gather(0)
     gather(1)
-    for n in range(1, 4):
+    gather_on(0)
+    for n in range(1, 3):
         loads[n].wait()
+    gather(2)
+    gather_on(1)
     compute(0)
-    gather(2)
+    gather(3)
+    gather_on(2)
     compute(1)
-    gather(3)
+    gather_on(3)
+    sum_on(0)
+    compute(2)
+    sum_on(1)
     give_back(0)
-    compute(2)
+    compute(3)
+    sum_on(2)
     give_back(1)
-    compute(3)
+    sum_on(3)
     give_back(2)
     give_back(3)
 
@@ -223,7 +270,7 @@
         mixture = mixture + dot(high[:, c * crows : (c + 1) * crows], back)
         mixture = mixture + dot(low[:, c * crows : (c + 1) * crows], back)
     residual = mixed.astype(F32) + mixture
-    sout_ref[...] = residual.astype(BF)
+    residual_ref[...] = residual
     squares = residual * residual
     lanes = squares[:, 0:128]
     for n in range(1, quarter // 128):
@@ -234,9 +281,13 @@
 
     for j in range(1, HID):
         p_copy(j).wait_send()
-        for c in range(CHUNKS):
-            f_copy(j, c).wait_send()
-            s_copy(j, c).wait_send()
+    for c in range(CHUNKS):
+        for b in range(2):
+            f_copy(1 + 2 * b, c).wait_send()
+            f_pass(b, c).wait_send()
+            s_pass(b, c).wait_send()
+            s_copy(1, b, c).wait_send()
+            s_copy(3, b, c).wait_send()
     each(1, EXPERTS, lambda i: d_copy(i).wait_send())
     each(1, EXPERTS, lambda i: r_copy(i).wait_send())
 
@@ -244,7 +295,7 @@
         q_copy(j).wait_recv()
         lanes = lanes + sq[j]
     rms = jnp.sum(lanes, axis=1, keepdims=True) / (quarter * HID)
-    normed_ref[...] = (residual * lax.rsqrt(rms + EPSILON) * gain_ref[...]).astype(BF)
+    scaled_ref[...] = residual * lax.rsqrt(rms + EPSILON)
     for j in range(1, HID):
         q_copy(j).wait_send()
 
@@ -254,47 +305,45 @@
     full_width = quarter * HID
     width = gate_up.shape[3]
     rows = EXPERTS * MOST
-    gate = gate_up[0, :, 0, :]
-    up = gate_up[0, :, 1, :]
+    gate_up_t = gate_up[0].transpose(1, 2, 0).reshape(2 * width, full_width)
     down = down_proj[0]
     vmem = pl.BlockSpec(memory_space=pltpu.VMEM)
     hbm = pl.BlockSpec(memory_space=pl.ANY)
     dma = pltpu.SemaphoreType.DMA
-    return pl.pallas_call(
+    residual, scaled = pl.pallas_call(
         kernel,
         out_shape=(
-            jax.ShapeDtypeStruct((tok, quarter), BF),
-            jax.ShapeDtypeStruct((tok, quarter), BF),
+            jax.ShapeDtypeStruct((tok, quarter), F32),
+            jax.ShapeDtypeStruct((tok, quarter), F32),
         ),
-        in_specs=[vmem] * 5 + [hbm] * 4,
+        in_specs=[vmem] * 4 + [hbm] * 3,
         out_specs=(vmem, vmem),
         scratch_shapes=[
             pltpu.VMEM(o_weight.shape, BF),
-            pltpu.VMEM(gate.shape, BF),
-            pltpu.VMEM(up.shape, BF),
+            pltpu.VMEM(gate_up_t.shape, BF),
             pltpu.VMEM(down.shape, BF),
             pltpu.VMEM((HID, tok, quarter), BF),
             pltpu.VMEM((HID, tok, quarter), BF),
             pltpu.VMEM((rows, quarter), BF),
             pltpu.VMEM((HID, rows, quarter), BF),
             pltpu.VMEM((HID, rows, quarter), BF),
-            pltpu.VMEM((HID, rows, quarter), BF),
+            pltpu.VMEM((2, rows, quarter), BF),
+            pltpu.VMEM((rows, quarter), BF),
             pltpu.VMEM((rows, quarter), BF),
             pltpu.VMEM((rows, quarter), BF),
             pltpu.VMEM((HID, tok, 128), F32),
-            dma((4,)),
+            dma((3,)),
             dma((HID,)), dma((HID,)),
             dma((EXPERTS,)), dma((EXPERTS,)),
             dma((HID, CHUNKS)), dma((HID, CHUNKS)),
-            dma((HID, CHUNKS)), dma((HID, CHUNKS)),
+            dma((3, 2, CHUNKS)), dma((3, 2, CHUNKS)),
             dma((EXPERTS,)), dma((EXPERTS,)),
             dma((HID,)), dma((HID,)),
         ],
         compiler_params=pltpu.CompilerParams(collective_id=0, has_side_effects=True),
-    )(
-        attention, stream, routes, route_weight, norm_gain.reshape(1, quarter),
-        o_weight, gate, up, down,
-    )
+    )(attention, stream, routes.T, route_weight.T, o_weight, gate_up_t, down)
+    normed = (scaled * norm_gain[None, :]).astype(BF)
+    return residual.astype(BF), normed
 
 
 def solution(mesh):

time: 87.3 us -> 76.3 us (0.87)
  local copies, waits for them, and re-layouts: 8.52 us -> 0.01 us
  Pallas kernels: 77.5 us -> 72.1 us
  other arithmetic: 0 us -> 3.04 us
    unnamed x12 -> x2, local copies, waits for them, and re-layouts: 6.62 us -> 0.01 us
    pallas_call x1, Pallas kernels: 77.5 us -> 72.1 us  [on_device(): pl.pallas_call(kernel, out_shape=(jax.ShapeDtypeStruct((tok, quarter), F3...]
    convert_element_type x0 -> x2, other arithmetic: none -> 3.04 us  [the longest x1 1.52 us: on_device(): normed = (scaled * norm_gain[None, :]).astype(BF)]
    slice x1 -> x0, local copies, waits for them, and re-layouts: 1.32 us -> none  [on_device(): up = gate_up[0, :, 1, :]]
where the time goes in v2:
time: 76.3 us; the launch traced here: 75.8 us
  Pallas kernels  72.1 us (94%)
  other arithmetic  3.04 us (4%)
    pallas_call x1, Pallas kernels, on_device(): pl.pallas_call(kernel, out_shape=(jax.ShapeDtypeStruct((tok, quarter), F3...  72.1 us

profile of v2, /device:TPU:1, one launch (start us, length us, event | category | flops | bytes accessed | tf_op | source)
XLA Modules:
  0.0 75.8 jit_solution(958689503304267772)
XLA Ops:
  0.6 0.0 copy-start
  0.6 72.1 %shard_map.95 = (f32[64,384]{1,0:T(8,128)}, f32[64,384]{1,0:T(8,128)}) custom-call(bf16[64,384]{1,0:T(8,128)(2,1)} %att_ref.1, bf16[64,384]{1,0:T(8,128)(2,1)} %stream_ref.1, s32[4,64]{1,0:T(4,128)} %bitcast.10, f32[4,64]{1,0:T(4,128)} %bitcast.11, bf16[384,1536]{1,0:T(8,128)(2,1)} %ow_hbm.1, bf16[384,1536]{1,0:T(8,128)(2,1)} %bitcast.8, ...), custom_call_target="tpu_custom_call" | custom-call | tf_op jit(solution)/shard_map/pallas_call | solution.py:313
  72.8 1.5 %convert_element_type.6 = bf16[64,384]{1,0:T(8,128)(2,1)} convert(f32[64,384]{1,0:T(8,128)} %get-tuple-element.4) | non-fusion elementwise | flops 24576 | bytes 147456 | tf_op jit(solution)/shard_map/convert_element_type | solution.py:346
  74.3 0.0 copy-done
  74.3 1.5 %multiply_convert_fusion = bf16[64,384]{1,0:T(8,128)(2,1)} fusion(f32[64,384]{1,0:T(8,128)} %get-tuple-element.5, f32[384]{0:T(512)S(1)} %copy-done), kind=kLoop, calls=%fused_computation | loop fusion | flops 49152 | bytes 148992 | tf_op jit(solution)/shard_map/convert_element_type | solution.py:345
Async XLA Ops:
  0.6 73.7 %copy-start = (f32[384]{0:T(512)S(1)}, f32[384]{0:T(512)}, u32[]{:S(2)}) copy-start(f32[384]{0:T(512)} %param.15) | copy-start | bytes 4612

commit v3 on v2

--- a/solution.py
+++ b/solution.py
@@ -24,7 +24,7 @@
 
 def kernel(
     att_ref, stream_ref, routes_ref, rw_ref, ow_hbm, gu_hbm, down_hbm,
-    residual_ref, scaled_ref,
+    residual_ref, inverse_ref,
     ow_v, gu_v, down_v, proj, projr, outg, full, part, partr, passing, res, ret, sq,
     w_sem, p_send, p_recv, d_send, d_recv, f_send, f_recv, s_send, s_recv, r_send, r_recv,
     q_send, q_recv,
@@ -35,16 +35,27 @@
     base = me - loc
     tok, quarter = stream_ref.shape
     rows = EXPERTS * MOST
-    shifts = EXPERTS // CHUNKS
     crows = rows // CHUNKS
     hrows = crows // 2
     width = gu_v.shape[0] // 2
 
-    def ahead(i):
-        return base + lax.rem(loc + i, EXPERTS)
-
-    def behind(i):
-        return base + lax.rem(loc + EXPERTS - i, EXPERTS)
+    core, zed, why = lax.rem(loc, 2), lax.rem(loc // 2, 8), loc // 16
+
+    def distance(c, b):
+        near = (1, 0, 3, 2)[c]
+        return near if b == 0 else (4 if c == 1 else 8 - near)
+
+    def ahead(c, b, q):
+        return (
+            base + 16 * lax.rem(why + q // 2, 2) + 2 * lax.rem(zed + distance(c, b), 8)
+            + lax.rem(core + q % 2, 2)
+        )
+
+    def behind(c, b, q):
+        return (
+            base + 16 * lax.rem(why + q // 2, 2) + 2 * lax.rem(zed + 8 - distance(c, b), 8)
+            + lax.rem(core + q % 2, 2)
+        )
 
     def hid_up(j):
         return lax.rem(hid + j, HID)
@@ -74,7 +85,7 @@
 
     def greet(i, carry):
         pl.semaphore_signal(
-            barrier, inc=1, device_id={"ep": ahead(i), "hid": hid},
+            barrier, inc=1, device_id={"ep": base + lax.rem(loc + i, EXPERTS), "hid": hid},
             device_id_type=pl.DeviceIdType.MESH,
         )
         return carry
@@ -125,29 +136,33 @@
     def q_copy(j):
         return over_hid(sq.at[0], sq.at[j], q_send.at[j], q_recv.at[j], j)
 
-    def d_copy(i):
-        return pltpu.make_async_remote_copy(
-            src_ref=outg.at[slot(i)], dst_ref=full.at[0, slot(i)],
-            send_sem=d_send.at[i], recv_sem=d_recv.at[i],
-            device_id={"ep": ahead(i), "hid": hid}, device_id_type=pl.DeviceIdType.MESH,
-        )
-
-    def r_copy(i):
-        return pltpu.make_async_remote_copy(
-            src_ref=res.at[slot(i)], dst_ref=ret.at[slot(i)],
-            send_sem=r_send.at[i], recv_sem=r_recv.at[i],
-            device_id={"ep": behind(i), "hid": hid}, device_id_type=pl.DeviceIdType.MESH,
-        )
-
-    def each(low, high, act):
-        def body(i, carry):
-            act(i)
+    def d_copy(c, b, q):
+        n = c * 8 + b * 4 + q
+        return pltpu.make_async_remote_copy(
+            src_ref=outg.at[slot(n)], dst_ref=full.at[0, slot(n)],
+            send_sem=d_send.at[n], recv_sem=d_recv.at[n],
+            device_id={"ep": ahead(c, b, q), "hid": hid}, device_id_type=pl.DeviceIdType.MESH,
+        )
+
+    def r_copy(c, b, q):
+        n = c * 8 + b * 4 + q
+        return pltpu.make_async_remote_copy(
+            src_ref=res.at[slot(n)], dst_ref=ret.at[slot(n)],
+            send_sem=r_send.at[n], recv_sem=r_recv.at[n],
+            device_id={"ep": behind(c, b, q), "hid": hid}, device_id_type=pl.DeviceIdType.MESH,
+        )
+
+    def each(c, act):
+        def both(q, carry):
+            act(c, 0, q)
+            act(c, 1, q)
             return carry
 
-        lax.fori_loop(low, high, body, 0)
-
-    def span(c):
-        return max(1, c * shifts), (c + 1) * shifts
+        if c == 1:
+            act(c, 1, 0)
+        lax.fori_loop(1 if c == 1 else 0, 4, both, 0)
+
+    own = pl.ds(crows, MOST)
 
     att = att_ref[...]
     loads[0].wait()
@@ -158,7 +173,13 @@
         p_copy(j).start()
 
     row = lax.broadcasted_iota(jnp.int32, (rows, tok), 0)
-    expert = (loc + row // MOST) % EXPERTS
+    number = row // MOST
+    near = (number // 8) ^ 1
+    far = jnp.where(number // 8 == 1, 4, 8 - near)
+    step = jnp.where((number // 4) % 2 == 0, near, far)
+    expert = (
+        16 * ((why + (number % 4) // 2) % 2) + 2 * ((zed + step) % 8) + (core + number) % 2
+    )
     place = (row % MOST).astype(F32)
     named = jnp.zeros((rows, tok), F32)
     weight = jnp.zeros((rows, tok), F32)
@@ -188,12 +209,12 @@
     for c in range(CHUNKS):
         block = dot(pick[c * crows : (c + 1) * crows], mixed).astype(BF)
         outg[chunk(c)] = block
-        if c == 0:
-            full[0, 0:MOST] = block[0:MOST]
-        each(*span(c), lambda i: d_copy(i).start())
+        if c == 1:
+            full[0, own] = block[0:MOST]
+        each(c, lambda *n: d_copy(*n).start())
 
     def gather(c):
-        each(*span(c), lambda i: d_copy(i).wait_recv())
+        each(c, lambda *n: d_copy(*n).wait_recv())
         for j in (1, 3):
             f_copy(j, c).start()
 
@@ -236,36 +257,36 @@
         value = part[0, chunk(c)].astype(F32) + partr[0, chunk(c)].astype(F32)
         value = (value + partr[1, chunk(c)].astype(F32)).astype(BF)
         res[chunk(c)] = value
-        if c == 0:
-            ret[0:MOST] = value[0:MOST]
-        each(*span(c), lambda i: r_copy(i).start())
+        if c == 1:
+            ret[own] = value[0:MOST]
+        each(c, lambda *n: r_copy(*n).start())
 
     gather(0)
-    gather(1)
-    gather_on(0)
     for n in range(1, 3):
         loads[n].wait()
+    gather_on(0)
+    gather(1)
+    compute(0)
+    gather_on(1)
     gather(2)
-    gather_on(1)
-    compute(0)
+    sum_on(0)
+    compute(1)
+    gather_on(2)
     gather(3)
-    gather_on(2)
-    compute(1)
+    give_back(0)
+    sum_on(1)
+    compute(2)
     gather_on(3)
-    sum_on(0)
-    compute(2)
-    sum_on(1)
-    give_back(0)
+    give_back(1)
+    sum_on(2)
     compute(3)
-    sum_on(2)
-    give_back(1)
+    give_back(2)
     sum_on(3)
-    give_back(2)
     give_back(3)
 
     mixture = jnp.zeros((tok, quarter), F32)
     for c in range(CHUNKS):
-        each(*span(c), lambda i: r_copy(i).wait_recv())
+        each(c, lambda *n: r_copy(*n).wait_recv())
         back = ret[chunk(c)]
         mixture = mixture + dot(high[:, c * crows : (c + 1) * crows], back)
         mixture = mixture + dot(low[:, c * crows : (c + 1) * crows], back)
@@ -288,14 +309,15 @@
             s_pass(b, c).wait_send()
             s_copy(1, b, c).wait_send()
             s_copy(3, b, c).wait_send()
-    each(1, EXPERTS, lambda i: d_copy(i).wait_send())
-    each(1, EXPERTS, lambda i: r_copy(i).wait_send())
+    for c in range(CHUNKS):
+        each(c, lambda *n: d_copy(*n).wait_send())
+        each(c, lambda *n: r_copy(*n).wait_send())
 
     for j in range(1, HID):
         q_copy(j).wait_recv()
         lanes = lanes + sq[j]
     rms = jnp.sum(lanes, axis=1, keepdims=True) / (quarter * HID)
-    scaled_ref[...] = residual * lax.rsqrt(rms + EPSILON)
+    inverse_ref[...] = jnp.broadcast_to(lax.rsqrt(rms + EPSILON), residual.shape)
     for j in range(1, HID):
         q_copy(j).wait_send()
 
@@ -310,7 +332,7 @@
     vmem = pl.BlockSpec(memory_space=pltpu.VMEM)
     hbm = pl.BlockSpec(memory_space=pl.ANY)
     dma = pltpu.SemaphoreType.DMA
-    residual, scaled = pl.pallas_call(
+    residual, inverse = pl.pallas_call(
         kernel,
         out_shape=(
             jax.ShapeDtypeStruct((tok, quarter), F32),
@@ -342,7 +364,7 @@
         ],
         compiler_params=pltpu.CompilerParams(collective_id=0, has_side_effects=True),
     )(attention, stream, routes.T, route_weight.T, o_weight, gate_up_t, down)
-    normed = (scaled * norm_gain[None, :]).astype(BF)
+    normed = (residual * inverse * norm_gain[None, :]).astype(BF)
     return residual.astype(BF), normed
 
 

time: 76.3 us -> 75.9 us (level)
  other arithmetic: 3.04 us -> 1.64 us
  Pallas kernels: 72.1 us -> 73.4 us
    convert_element_type x2 -> x1, other arithmetic: 3.04 us -> 1.64 us  [on_device(): normed = (residual * inverse * norm_gain[None, :]).astype(BF)]
    pallas_call x1, Pallas kernels: 72.1 us -> 73.4 us  [on_device(): pl.pallas_call(kernel, out_shape=(jax.ShapeDtypeStruct((tok, quarter), F3...]
where the time goes in v3:
time: 75.9 us; the launch traced here: 75.7 us
  Pallas kernels  73.4 us (97%)
  other arithmetic  1.64 us (2%)
    pallas_call x1, Pallas kernels, on_device(): pl.pallas_call(kernel, out_shape=(jax.ShapeDtypeStruct((tok, quarter), F3...  73.4 us
    convert_element_type x1, other arithmetic, on_device(): normed = (residual * inverse * norm_gain[None, :]).astype(BF)  1.64 us

profile of v3, /device:TPU:1, one launch (start us, length us, event | category | flops | bytes accessed | tf_op | source)
XLA Modules:
  0.0 75.7 jit_solution(14734381629246328609)
XLA Ops:
  0.6 0.0 copy-start
  0.6 73.4 %shard_map.95 = (f32[64,384]{1,0:T(8,128)}, f32[64,384]{1,0:T(8,128)}) custom-call(bf16[64,384]{1,0:T(8,128)(2,1)} %att_ref.1, bf16[64,384]{1,0:T(8,128)(2,1)} %stream_ref.1, s32[4,64]{1,0:T(4,128)} %bitcast.10, f32[4,64]{1,0:T(4,128)} %bitcast.11, bf16[384,1536]{1,0:T(8,128)(2,1)} %ow_hbm.1, bf16[384,1536]{1,0:T(8,128)(2,1)} %bitcast.8, ...), custom_call_target="tpu_custom_call" | custom-call | tf_op jit(solution)/shard_map/pallas_call | solution.py:335
  74.1 0.0 copy-done
  74.1 1.6 %multiply_convert_fusion = (bf16[64,384]{1,0:T(8,128)(2,1)}, bf16[64,384]{1,0:T(8,128)(2,1)}) fusion(f32[64,384]{1,0:T(8,128)} %get-tuple-element.4, f32[64,384]{1,0:T(8,128)} %get-tuple-element.5, f32[384]{0:T(512)S(1)} %copy-done), kind=kLoop, calls=%fused_computation | loop fusion | flops 98304 | bytes 296448 | tf_op jit(solution)/shard_map/convert_element_type | solution.py:367
Async XLA Ops:
  0.6 73.4 %copy-start = (f32[384]{0:T(512)S(1)}, f32[384]{0:T(512)}, u32[]{:S(2)}) copy-start(f32[384]{0:T(512)} %param.15) | copy-start | bytes 4612

commit v4 on v3

--- a/solution.py
+++ b/solution.py
@@ -64,7 +64,7 @@
         return pl.ds(pl.multiple_of(hid_up(j) * quarter, quarter), quarter)
 
     def slot(i):
-        return pl.ds(pl.multiple_of(i * MOST, MOST), MOST)
+        return pl.ds(i * MOST, MOST)
 
     def chunk(c):
         return pl.ds(c * crows, crows)
@@ -140,7 +140,7 @@
         n = c * 8 + b * 4 + q
         return pltpu.make_async_remote_copy(
             src_ref=outg.at[slot(n)], dst_ref=full.at[0, slot(n)],
-            send_sem=d_send.at[n], recv_sem=d_recv.at[n],
+            send_sem=d_send.at[c], recv_sem=d_recv.at[c],
             device_id={"ep": ahead(c, b, q), "hid": hid}, device_id_type=pl.DeviceIdType.MESH,
         )
 
@@ -148,21 +148,33 @@
         n = c * 8 + b * 4 + q
         return pltpu.make_async_remote_copy(
             src_ref=res.at[slot(n)], dst_ref=ret.at[slot(n)],
-            send_sem=r_send.at[n], recv_sem=r_recv.at[n],
+            send_sem=r_send.at[c], recv_sem=r_recv.at[c],
             device_id={"ep": behind(c, b, q), "hid": hid}, device_id_type=pl.DeviceIdType.MESH,
         )
 
     def each(c, act):
-        def both(q, carry):
-            act(c, 0, q)
-            act(c, 1, q)
-            return carry
-
-        if c == 1:
-            act(c, 1, 0)
-        lax.fori_loop(1 if c == 1 else 0, 4, both, 0)
+        for q in range(4):
+            for b in range(2):
+                if (c, b, q) != (1, 0, 0):
+                    act(c, b, q)
 
     own = pl.ds(crows, MOST)
+
+    def d_all(c):
+        part_rows = pl.ds(c * crows, crows - MOST if c == 1 else crows)
+        return pltpu.make_async_remote_copy(
+            src_ref=outg.at[part_rows], dst_ref=full.at[0, part_rows],
+            send_sem=d_send.at[c], recv_sem=d_recv.at[c],
+            device_id={"ep": ahead(c, 1, 0), "hid": hid}, device_id_type=pl.DeviceIdType.MESH,
+        )
+
+    def r_all(c):
+        part_rows = pl.ds(c * crows, crows - MOST if c == 1 else crows)
+        return pltpu.make_async_remote_copy(
+            src_ref=res.at[part_rows], dst_ref=ret.at[part_rows],
+            send_sem=r_send.at[c], recv_sem=r_recv.at[c],
+            device_id={"ep": behind(c, 1, 0), "hid": hid}, device_id_type=pl.DeviceIdType.MESH,
+        )
 
     att = att_ref[...]
     loads[0].wait()
@@ -214,7 +226,7 @@
         each(c, lambda *n: d_copy(*n).start())
 
     def gather(c):
-        each(c, lambda *n: d_copy(*n).wait_recv())
+        d_all(c).wait_recv()
         for j in (1, 3):
             f_copy(j, c).start()
 
@@ -286,7 +298,7 @@
 
     mixture = jnp.zeros((tok, quarter), F32)
     for c in range(CHUNKS):
-        each(c, lambda *n: r_copy(*n).wait_recv())
+        r_all(c).wait_recv()
         back = ret[chunk(c)]
         mixture = mixture + dot(high[:, c * crows : (c + 1) * crows], back)
         mixture = mixture + dot(low[:, c * crows : (c + 1) * crows], back)
@@ -310,8 +322,8 @@
             s_copy(1, b, c).wait_send()
             s_copy(3, b, c).wait_send()
     for c in range(CHUNKS):
-        each(c, lambda *n: d_copy(*n).wait_send())
-        each(c, lambda *n: r_copy(*n).wait_send())
+        d_all(c).wait_send()
+        r_all(c).wait_send()
 
     for j in range(1, HID):
         q_copy(j).wait_recv()
@@ -356,10 +368,10 @@
             pltpu.VMEM((HID, tok, 128), F32),
             dma((3,)),
             dma((HID,)), dma((HID,)),
-            dma((EXPERTS,)), dma((EXPERTS,)),
+            dma((CHUNKS,)), dma((CHUNKS,)),
             dma((HID, CHUNKS)), dma((HID, CHUNKS)),
             dma((3, 2, CHUNKS)), dma((3, 2, CHUNKS)),
-            dma((EXPERTS,)), dma((EXPERTS,)),
+            dma((CHUNKS,)), dma((CHUNKS,)),
             dma((HID,)), dma((HID,)),
         ],
         compiler_params=pltpu.CompilerParams(collective_id=0, has_side_effects=True),

time: 75.9 us -> 74.4 us (0.980)
  Pallas kernels: 73.4 us -> 71.8 us
    pallas_call x1, Pallas kernels: 73.4 us -> 71.8 us  [on_device(): pl.pallas_call(kernel, out_shape=(jax.ShapeDtypeStruct((tok, quarter), F3...]
where the time goes in v4:
time: 74.4 us; the launch traced here: 74.1 us
  Pallas kernels  71.8 us (97%)
  other arithmetic  1.64 us (2%)
    pallas_call x1, Pallas kernels, on_device(): pl.pallas_call(kernel, out_shape=(jax.ShapeDtypeStruct((tok, quarter), F3...  71.8 us
    convert_element_type x1, other arithmetic, on_device(): normed = (residual * inverse * norm_gain[None, :]).astype(BF)  1.64 us

profile of v4, /device:TPU:1, one launch (start us, length us, event | category | flops | bytes accessed | tf_op | source)
XLA Modules:
  0.0 74.1 jit_solution(3222776224393988998)
XLA Ops:
  0.6 0.0 copy-start
  0.6 71.8 %shard_map.95 = (f32[64,384]{1,0:T(8,128)}, f32[64,384]{1,0:T(8,128)}) custom-call(bf16[64,384]{1,0:T(8,128)(2,1)} %att_ref.1, bf16[64,384]{1,0:T(8,128)(2,1)} %stream_ref.1, s32[4,64]{1,0:T(4,128)} %bitcast.10, f32[4,64]{1,0:T(4,128)} %bitcast.11, bf16[384,1536]{1,0:T(8,128)(2,1)} %ow_hbm.1, bf16[384,1536]{1,0:T(8,128)(2,1)} %bitcast.8, ...), custom_call_target="tpu_custom_call" | custom-call | tf_op jit(solution)/shard_map/pallas_call | solution.py:347
  72.5 0.0 copy-done
  72.5 1.6 %multiply_convert_fusion = (bf16[64,384]{1,0:T(8,128)(2,1)}, bf16[64,384]{1,0:T(8,128)(2,1)}) fusion(f32[64,384]{1,0:T(8,128)} %get-tuple-element.4, f32[64,384]{1,0:T(8,128)} %get-tuple-element.5, f32[384]{0:T(512)S(1)} %copy-done), kind=kLoop, calls=%fused_computation | loop fusion | flops 98304 | bytes 296448 | tf_op jit(solution)/shard_map/convert_element_type | solution.py:379
Async XLA Ops:
  0.6 71.8 %copy-start = (f32[384]{0:T(512)S(1)}, f32[384]{0:T(512)}, u32[]{:S(2)}) copy-start(f32[384]{0:T(512)} %param.15) | copy-start | bytes 4612

commit v5 on v4

--- a/solution.py
+++ b/solution.py
@@ -305,10 +305,9 @@
     residual = mixed.astype(F32) + mixture
     residual_ref[...] = residual
     squares = residual * residual
-    lanes = squares[:, 0:128]
-    for n in range(1, quarter // 128):
-        lanes = lanes + squares[:, n * 128 : (n + 1) * 128]
-    sq[0] = lanes
+    sums = jnp.broadcast_to(jnp.sum(squares, axis=1, keepdims=True), (tok, 128))
+    sums = jnp.concatenate([sums] * (128 // tok), axis=0).T[0:8]
+    sq[0] = sums
     for j in (2, 1, 3):
         q_copy(j).start()
 
@@ -327,8 +326,8 @@
 
     for j in range(1, HID):
         q_copy(j).wait_recv()
-        lanes = lanes + sq[j]
-    rms = jnp.sum(lanes, axis=1, keepdims=True) / (quarter * HID)
+        sums = sums + sq[j]
+    rms = sums.T[0:tok, 0:1] / (quarter * HID)
     inverse_ref[...] = jnp.broadcast_to(lax.rsqrt(rms + EPSILON), residual.shape)
     for j in range(1, HID):
         q_copy(j).wait_send()
@@ -365,7 +364,7 @@
             pltpu.VMEM((rows, quarter), BF),
             pltpu.VMEM((rows, quarter), BF),
             pltpu.VMEM((rows, quarter), BF),
-            pltpu.VMEM((HID, tok, 128), F32),
+            pltpu.VMEM((HID, 8, 128), F32),
             dma((3,)),
             dma((HID,)), dma((HID,)),
             dma((CHUNKS,)), dma((CHUNKS,)),

time: 74.4 us -> 73.7 us (level)
  no operation moved by 1% of the time
where the time goes in v5:
time: 73.7 us; the launch traced here: 73.5 us
  Pallas kernels  71.2 us (97%)
  other arithmetic  1.64 us (2%)
    pallas_call x1, Pallas kernels, on_device(): pl.pallas_call(kernel, out_shape=(jax.ShapeDtypeStruct((tok, quarter), F3...  71.2 us
    convert_element_type x1, other arithmetic, on_device(): normed = (residual * inverse * norm_gain[None, :]).astype(BF)  1.64 us

profile of v5, /device:TPU:1, one launch (start us, length us, event | category | flops | bytes accessed | tf_op | source)
XLA Modules:
  0.0 73.5 jit_solution(14576894583142571358)
XLA Ops:
  0.6 0.0 copy-start
  0.6 71.2 %shard_map.95 = (f32[64,384]{1,0:T(8,128)}, f32[64,384]{1,0:T(8,128)}) custom-call(bf16[64,384]{1,0:T(8,128)(2,1)} %att_ref.1, bf16[64,384]{1,0:T(8,128)(2,1)} %stream_ref.1, s32[4,64]{1,0:T(4,128)} %bitcast.10, f32[4,64]{1,0:T(4,128)} %bitcast.11, bf16[384,1536]{1,0:T(8,128)(2,1)} %ow_hbm.1, bf16[384,1536]{1,0:T(8,128)(2,1)} %bitcast.8, ...), custom_call_target="tpu_custom_call" | custom-call | tf_op jit(solution)/shard_map/pallas_call | solution.py:346
  71.8 0.0 copy-done
  71.8 1.6 %multiply_convert_fusion = (bf16[64,384]{1,0:T(8,128)(2,1)}, bf16[64,384]{1,0:T(8,128)(2,1)}) fusion(f32[64,384]{1,0:T(8,128)} %get-tuple-element.4, f32[64,384]{1,0:T(8,128)} %get-tuple-element.5, f32[384]{0:T(512)S(1)} %copy-done), kind=kLoop, calls=%fused_computation | loop fusion | flops 98304 | bytes 296448 | tf_op jit(solution)/shard_map/convert_element_type | solution.py:378
Async XLA Ops:
  0.6 71.2 %copy-start = (f32[384]{0:T(512)S(1)}, f32[384]{0:T(512)}, u32[]{:S(2)}) copy-start(f32[384]{0:T(512)} %param.15) | copy-start | bytes 4612
